TPU v7x, 128 devices: a whole 4x4x4 slice. The times are simulated.
128 devices in a mesh: dp: 8 (over x, core), space: 16 (over y, z).
Axes of the slice: x: 4, y: 4, z: 4, core: 2. Of those that a mesh axis runs over, the one named last changes fastest.
Arguments:
- layer_input: bfloat16 [8, 64, 32, 1024], P('dp', None, 'space'), may hold values from -6 to 6
- hidden_pre: bfloat16 [8, 128, 32, 1024], P('dp', None, 'space'), may hold values from -6 to 6
- output_pre: bfloat16 [8, 256, 16, 256], P('dp', None, 'space'), may hold values from -6 to 6
- output_grad: bfloat16 [8, 256, 16, 256], P('dp', None, 'space'), may hold values from -48 to 48
- weight_a: bfloat16 [27, 64, 128], replicated, may hold values from -0.15625 to 0.15625
- weight_b: bfloat16 [27, 128, 256], replicated, may hold values from -0.109375 to 0.109375
Outputs:
- input_grad: bfloat16 [8, 64, 32, 1024], P('dp', None, 'space')
- weight_grad_a: float32 [27, 64, 128], replicated
- weight_grad_b: float32 [27, 128, 256], replicated
All inputs are finite; a program needn't handle non-finite values.
Results may differ from a plain program's by a relative error of at most 0.013.
Values may be sent and summed in bfloat16 or wider, within the bound.
A program may use at most 64 MiB of HBM per device.

v0:
```python
import math

import jax
import jax.numpy as jnp
from jax import lax
from jax.sharding import PartitionSpec as P

negative_slope = 0.3


def padded_2(cells, sides, width):
    for axis, dim in sides:
        count = lax.axis_size(axis)
        ends = count - 1
        head = lax.slice_in_dim(cells, 0, width, axis=dim)
        tail = lax.slice_in_dim(cells, cells.shape[dim] - width, cells.shape[dim], axis=dim)
        cells = jnp.concatenate(
            [
                lax.ppermute(tail, axis, [(i, (i + 1) % count) for i in range(ends)]),
                cells,
                lax.ppermute(head, axis, [((i + 1) % count, i) for i in range(ends)]),
            ],
            axis=dim,
        )
    return cells


def slopes(values):
    return jnp.where(values > 0, jnp.ones_like(values), negative_slope * jnp.ones_like(values))


def window(padded, tap_z, tap_y, tap_x, depth, side):
    planes = padded[:, tap_z : tap_z + depth, :]
    margin = side + 1
    wider = jnp.pad(planes, ((0, 0), (0, 0), (margin, margin)))
    offset = (tap_y - 1) * side + (tap_x - 1)
    piece = wider[:, :, margin + offset : margin + offset + side * side]
    column = jnp.arange(side * side, dtype=jnp.int32) % side + (tap_x - 1)
    inside = (column >= 0) & (column < side)
    piece = jnp.where(inside, piece, jnp.zeros_like(piece))
    return piece.reshape(padded.shape[0], depth * side * side)


def outer_product(left, right):
    return lax.dot_general(
        left, right, (((1,), (1,)), ((), ())), preferred_element_type=jnp.float32
    )


def per_device(layer_input, hidden_pre, output_pre, output_grad, weight_a, weight_b):
    side = math.isqrt(layer_input.shape[3])
    half = side // 2
    depth_a = layer_input.shape[2]
    depth_b = depth_a // 2
    source = layer_input[0]
    hidden = hidden_pre[0]
    outer = output_pre[0]
    upstream = output_grad[0]
    chan_in = source.shape[0]
    width_a = hidden.shape[0]
    width_b = outer.shape[0]
    grad_outer = (upstream.astype(jnp.float32) * slopes(outer.astype(jnp.float32))).astype(
        jnp.bfloat16
    )
    hidden_f = hidden.astype(jnp.float32)
    active = jnp.where(hidden_f > 0, hidden_f, negative_slope * hidden_f)
    pooled = (
        active.reshape(width_a, depth_b, 2, half, 2, half, 2)
        .mean(axis=(2, 4, 6))
        .astype(jnp.bfloat16)
    )
    pooled = pooled.reshape(width_a, depth_b, half * half)
    outer_pad = padded_2(grad_outer, (("space", 1),), 1)
    pooled_pad = padded_2(pooled, (("space", 1),), 1)
    grad_flat = grad_outer.reshape(width_b, depth_b * half * half)
    back_b = jnp.zeros((width_a, depth_b * half * half), jnp.float32)
    terms_b = []
    for tap in range(27):
        tap_z, tap_y, tap_x = (tap // 9, tap // 3 % 3, tap % 3)
        mirror = window(outer_pad, 2 - tap_z, 2 - tap_y, 2 - tap_x, depth_b, half)
        back_b = back_b + jnp.dot(weight_b[tap], mirror, preferred_element_type=jnp.float32)
        terms_b.append(
            outer_product(window(pooled_pad, tap_z, tap_y, tap_x, depth_b, half), grad_flat)
        )
    sums_b = jnp.stack(terms_b)
    coarse = back_b.reshape(width_a, depth_b, half, half)
    upward = jnp.repeat(jnp.repeat(jnp.repeat(coarse, 2, 1), 2, 2), 2, 3) * 0.125
    upward = upward.reshape(width_a, depth_a * side * side)
    grad_hidden = (upward * slopes(hidden_f.reshape(width_a, depth_a * side * side))).astype(
        jnp.bfloat16
    )
    grad_hidden = grad_hidden.reshape(width_a, depth_a, side * side)
    hidden_pad = padded_2(grad_hidden, (("space", 1),), 1)
    source_pad = padded_2(source, (("space", 1),), 1)
    hidden_flat = grad_hidden.reshape(width_a, depth_a * side * side)
    back_a = jnp.zeros((chan_in, depth_a * side * side), jnp.float32)
    terms_a = []
    for tap in range(27):
        tap_z, tap_y, tap_x = (tap // 9, tap // 3 % 3, tap % 3)
        mirror = window(hidden_pad, 2 - tap_z, 2 - tap_y, 2 - tap_x, depth_a, side)
        back_a = back_a + jnp.dot(weight_a[tap], mirror, preferred_element_type=jnp.float32)
        terms_a.append(
            outer_product(window(source_pad, tap_z, tap_y, tap_x, depth_a, side), hidden_flat)
        )
    sums_a = jnp.stack(terms_a)
    input_grad = back_a.astype(jnp.bfloat16).reshape(1, chan_in, depth_a, side * side)
    total_a, total_b = lax.psum((sums_a, sums_b), ("dp", "space"))
    samples = lax.axis_size("dp")
    planes_a = depth_a * lax.axis_size("space")
    scale_a = 1.0 / math.sqrt(samples * planes_a * side * side)
    scale_b = 1.0 / math.sqrt(samples * (planes_a // 2) * half * half)
    return (input_grad, total_a * scale_a, total_b * scale_b)


def solution(mesh):
    in_specs = (
        P("dp", None, "space", None),
        P("dp", None, "space", None),
        P("dp", None, "space", None),
        P("dp", None, "space", None),
        P(),
        P(),
    )
    out_specs = (P("dp", None, "space", None), P(), P())
    return jax.shard_map(
        per_device, mesh=mesh, in_specs=in_specs, out_specs=out_specs, check_vma=False
    )
```

profile of v0, /device:TPU:1, one launch (start us, length us, event | category | flops | bytes accessed | tf_op | source)
XLA Modules:
  0.0 248.0 jit_solution(2244934263055690898)
XLA Ops:
  7.2 1.1 multiply_convert_fusion.1
  8.3 4.4 %collective-permute-start.1 = (bf16[256,1,256]{2,0,1:T(8,128)(2,1)S(1)}, bf16[256,1,256]{2,0,1:T(8,128)(2,1)S(1)}, u32[]{:S(2)}, u32[]{:S(2)}) collective-permute-start(bf16[256,1,256]{2,0,1:T(8,128)(2,1)S(1)} %bitcast.918), channel_id=1, source_target_pairs={{0,1},{1,2},{2,3},{3,4},{4,5},{5,6},{6,7},{7,8},{8,9},{9,10},{10,1... | collective-permute-start | bytes 393224 | tf_op jit(solution)/shard_map/ppermute | solution.py:19
  12.7 1.3 collective-permute-start
  14.0 1.4 copy.37
  15.6 0.4 reduce_sum.18
  16.0 4.2 %collective-permute-start.6 = (bf16[128,1,256]{0,2,1:T(8,128)(2,1)S(1)}, bf16[128,1,256]{0,2,1:T(8,128)(2,1)S(1)}, u32[]{:S(2)}, u32[]{:S(2)}) collective-permute-start(bf16[128,1,256]{0,2,1:T(8,128)(2,1)S(1)} %bitcast.928), channel_id=1, source_target_pairs={{0,1},{1,2},{2,3},{3,4},{4,5},{5,6},{6,7},{7,8},{8,9},{9,10},{10,1... | collective-permute-start | bytes 196616 | tf_op jit(solution)/shard_map/ppermute | solution.py:19
  20.2 1.3 collective-permute-start.7
  21.5 1.2 fusion.578
  22.6 1.3 collective-permute-start.5
  24.2 1.3 broadcast_select_fusion.7
  26.0 4.6 %collective-permute-start.4 = (bf16[64,1,1024]{2,1,0:T(2,128)(2,1)}, bf16[64,1,1024]{2,1,0:T(2,128)(2,1)S(1)}, u32[]{:S(2)}, u32[]{:S(2)}) collective-permute-start(bf16[64,1,1024]{2,1,0:T(2,128)(2,1)} %get-tuple-element.96), channel_id=1, source_target_pairs={{0,1},{1,2},{2,3},{3,4},{4,5},{5,6},{6,7},{7,8},{8,9},{9,10},{10,1... | collective-permute-start | bytes 393224 | tf_op jit(solution)/shard_map/ppermute | solution.py:19
  38.4 0.3 fusion.96
  38.7 0.3 fusion.86
  39.0 0.3 convolution_add_fusion.30
  39.3 0.3 convolution_add_fusion.29
  39.6 0.3 convolution_add_fusion.28
  40.2 0.3 convolution_add_fusion.26
  40.5 0.3 convolution_add_fusion.25
  40.8 0.3 convolution_add_fusion.24
  41.1 0.3 convolution_add_fusion.23
  41.5 0.3 convolution_add_fusion.22
  41.8 0.3 convolution_add_fusion.21
  42.1 0.3 convolution_add_fusion.20
  42.6 0.3 convolution_add_fusion.18
  43.0 0.3 convolution_add_fusion.17
  43.3 0.3 fusion.48
  43.6 0.3 fusion.47
  43.9 0.3 convolution_bitcast_fusion.40
  44.2 0.3 fusion.46
  44.6 0.3 fusion.45
  44.9 0.3 fusion.44
  45.2 0.3 fusion.43
  45.7 0.3 fusion.41
  46.1 0.3 fusion.40
  46.4 0.3 fusion.51
  47.2 3.4 %collective-permute-start.3 = (bf16[128,1,1024]{0,2,1:T(8,128)(2,1)S(1)}, bf16[128,1,1024]{0,2,1:T(8,128)(2,1)S(1)}, u32[]{:S(2)}, u32[]{:S(2)}) collective-permute-start(bf16[128,1,1024]{0,2,1:T(8,128)(2,1)S(1)} %get-tuple-element.54), channel_id=1, source_target_pairs={{0,1},{1,2},{2,3},{3,4},{4,5},{5,6},{6,7},{7,8},{8,9},{9,10},{10,1... | collective-permute-start | bytes 786440 | tf_op jit(solution)/shard_map/ppermute | solution.py:19
  50.6 1.5 collective-permute-start.2
  52.1 4.2 %broadcast_select_fusion.14 = (bf16[64,2,1024]{2,1,0:T(2,128)(2,1)S(1)}, bf16[64,2,1024]{2,1,0:T(2,128)(2,1)S(1)}, bf16[64,2,1024]{2,1,0:T(2,128)(2,1)S(1)}, bf1...) fusion(pred[1024]{0:T(1024)(128)(4,1)S(1)} %fusion.521, ...), kind=kLoop, calls=%fused_computation.231 | loop fusion | flops 1966080 | bytes 2885632 | tf_op jit(solution)/shard_map/jit(_where)/select_n | solution.py:40
  56.3 2.9 %broadcast_select_fusion.10 = (bf16[64,2,1024]{2,1,0:T(2,128)(2,1)S(1)}, bf16[64,2,1024]{2,1,0:T(2,128)(2,1)S(1)}, bf16[64,2,1024]{2,1,0:T(2,128)(2,1)S(1)}, bf1...) fusion(pred[1024]{0:T(1024)(128)(4,1)S(1)} %get-tuple-element.1, ...), kind=kLoop, calls=%fused_computation.227 | loop fusion | flops 1048576 | bytes 2362368 | tf_op jit(solution)/shard_map/jit(_where)/select_n | solution.py:40
  60.0 2.9 %broadcast_select_fusion.4 = (bf16[64,2,1024]{2,1,0:T(2,128)(2,1)S(1)}, bf16[64,2,1024]{2,1,0:T(2,128)(2,1)S(1)}, bf16[64,2,1024]{2,1,0:T(2,128)(2,1)S(1)}, bf16...) fusion(pred[1024]{0:T(1024)(128)(4,1)S(1)} %get-tuple-element.1, ...), kind=kLoop, calls=%fused_computation.221 | loop fusion | flops 1048576 | bytes 2362368 | tf_op jit(solution)/shard_map/jit(_where)/select_n | solution.py:40
  63.4 1.2 broadcast_select_fusion
  70.7 0.9 copy-done.3
  71.7 2.5 %broadcast_select_fusion.1 = (bf16[128,2,1024]{0,2,1:T(8,128)(2,1)S(1)}, bf16[128,2,1024]{0,2,1:T(8,128)(2,1)S(1)}, bf16[128,2,1024]{0,2,1:T(8,128)(2,1)S(1)}, b...) fusion(pred[1024]{0:T(1024)(128)(4,1)S(1)} %fusion.521, ...), kind=kLoop, calls=%fused_computation.218 | loop fusion | flops 4718592 | bytes 7343104 | tf_op jit(solution)/shard_map/jit(_where)/select_n | solution.py:40
  74.2 3.7 %slice_select_fusion.16 = (bf16[128,2,1024]{0,2,1:T(8,128)(2,1)S(1)}, bf16[128,2,1024]{0,2,1:T(8,128)(2,1)S(1)}, bf16[128,2,1024]{0,2,1:T(8,128)(2,1)S(1)}, bf16...) fusion(pred[1024]{0:T(1024)(128)(4,1)S(1)} %get-tuple-element.1, ...), kind=kLoop, calls=%fused_computation.210 | loop fusion | flops 4194304 | bytes 9440256 | tf_op jit(solution)/shard_map/jit(_where)/select_n | solution.py:40
  78.2 0.3 convolution_add_fusion.15
  78.6 0.3 convolution_add_fusion.14
  78.9 0.3 convolution_add_fusion.13
  79.2 0.3 convolution_add_fusion.12
  79.5 0.3 convolution_add_fusion.11
  80.1 0.3 convolution_add_fusion.9
  80.4 0.3 convolution_add_fusion.8
  81.0 0.3 convolution_add_fusion.6
  81.3 0.3 convolution_add_fusion.5
  82.2 0.3 convolution_add_fusion.2
  82.5 0.3 convolution_add_fusion.1
  82.8 0.3 fusion.10
  84.3 0.3 fusion.5
  84.6 0.3 fusion.4
  85.2 0.3 fusion.2
  85.8 0.3 fusion.11
  86.1 0.9 reshape.926
  87.0 147.7 %all-reduce.15.cloned.1.call-done = (f32[27,64,128]{2,1,0:T(8,128)}, f32[27,128,256]{2,1,0:T(8,128)}) async-done(((f32[27,64,128]{2,1,0:T(8,128)}, f32[27,128,256]{2,1,0:T(8,128)}), (f32[27,64,128]{2,1,0:T(8,128)}, f32[27,128,256]{2,1,0:T(8,128)})) %all-reduce.15.cloned.1.call-update) | async-done | bytes 4423696 | tf_op jit(solution)/shard_map/psum | solution.py:107
  234.7 2.2 broadcast_multiply_fusion.1
  236.9 4.3 %broadcast_multiply_fusion = f32[27,128,256]{2,1,0:T(8,128)} fusion(f32[27,128,256]{2,1,0:T(8,128)} %get-tuple-element.4), kind=kLoop, calls=%fused_computation.38 | loop fusion | flops 884736 | bytes 7077888 | tf_op jit(solution)/shard_map/mul | solution.py:112
  (128 shorter events, 20.3 us)
Async XLA Ops:
  7.2 14.3 %copy-start = (bf16[1,64,2,1024]{3,2,1,0:T(2,128)(2,1)S(1)}, bf16[1,64,2,1024]{3,2,1,0:T(2,128)(2,1)}, u32[]{:S(2)}) copy-start(bf16[1,64,2,1024]{3,2,1,0:T(2,128)(2,1)} %param.6) | copy-start | bytes 786436
  7.2 227.5 %all-reduce.15.cloned.1.call-start = ((), (), s32[]{:S(2)}) async-start(), calls=%async_computation | async-start | bytes 8847360 | tf_op jit(solution)/shard_map/psum | solution.py:107
  8.3 35.6 %collective-permute-start.1 = (bf16[256,1,256]{2,0,1:T(8,128)(2,1)S(1)}, bf16[256,1,256]{2,0,1:T(8,128)(2,1)S(1)}, u32[]{:S(2)}, u32[]{:S(2)}) collective-permute-start(bf16[256,1,256]{2,0,1:T(8,128)(2,1)S(1)} %bitcast.918), channel_id=1, source_target_pairs={{0,1},{1,2},{2,3},{3,4},{4,5},{5,6},{6,7},{7,8},{8,9},{9,10},{10,1... | collective-permute-start | bytes 393224 | tf_op jit(solution)/shard_map/ppermute | solution.py:19
  12.7 25.7 %collective-permute-start = (bf16[256,1,256]{2,0,1:T(8,128)(2,1)S(1)}, bf16[256,1,256]{2,0,1:T(8,128)(2,1)S(1)}, u32[]{:S(2)}, u32[]{:S(2)}) collective-permute-start(bf16[256,1,256]{2,0,1:T(8,128)(2,1)S(1)} %bitcast.919), channel_id=1, source_target_pairs={{1,0},{2,1},{3,2},{4,3},{5,4},{6,5},{7,6},{8,7},{9,8},{10,9},{11,1... | collective-permute-start | bytes 393224 | tf_op jit(solution)/shard_map/ppermute | solution.py:21
  16.0 10.0 %collective-permute-start.6 = (bf16[128,1,256]{0,2,1:T(8,128)(2,1)S(1)}, bf16[128,1,256]{0,2,1:T(8,128)(2,1)S(1)}, u32[]{:S(2)}, u32[]{:S(2)}) collective-permute-start(bf16[128,1,256]{0,2,1:T(8,128)(2,1)S(1)} %bitcast.928), channel_id=1, source_target_pairs={{0,1},{1,2},{2,3},{3,4},{4,5},{5,6},{6,7},{7,8},{8,9},{9,10},{10,1... | collective-permute-start | bytes 196616 | tf_op jit(solution)/shard_map/ppermute | solution.py:19
  20.2 15.6 %collective-permute-start.7 = (bf16[128,1,256]{0,2,1:T(8,128)(2,1)S(1)}, bf16[128,1,256]{0,2,1:T(8,128)(2,1)S(1)}, u32[]{:S(2)}, u32[]{:S(2)}) collective-permute-start(bf16[128,1,256]{0,2,1:T(8,128)(2,1)S(1)} %bitcast.929), channel_id=1, source_target_pairs={{1,0},{2,1},{3,2},{4,3},{5,4},{6,5},{7,6},{8,7},{9,8},{10,9},{11,1... | collective-permute-start | bytes 196616 | tf_op jit(solution)/shard_map/ppermute | solution.py:21
  22.6 29.5 %collective-permute-start.5 = (bf16[64,1,1024]{2,1,0:T(2,128)(2,1)}, bf16[64,1,1024]{2,1,0:T(2,128)(2,1)}, u32[]{:S(2)}, u32[]{:S(2)}) collective-permute-start(bf16[64,1,1024]{2,1,0:T(2,128)(2,1)} %get-tuple-element.95), channel_id=1, source_target_pairs={{1,0},{2,1},{3,2},{4,3},{5,4},{6,5},{7,6},{8,7},{9,8},{10,9},{11,1... | collective-permute-start | bytes 393224 | tf_op jit(solution)/shard_map/ppermute | solution.py:21
  26.0 26.1 %collective-permute-start.4 = (bf16[64,1,1024]{2,1,0:T(2,128)(2,1)}, bf16[64,1,1024]{2,1,0:T(2,128)(2,1)S(1)}, u32[]{:S(2)}, u32[]{:S(2)}) collective-permute-start(bf16[64,1,1024]{2,1,0:T(2,128)(2,1)} %get-tuple-element.96), channel_id=1, source_target_pairs={{0,1},{1,2},{2,3},{3,4},{4,5},{5,6},{6,7},{7,8},{8,9},{9,10},{10,1... | collective-permute-start | bytes 393224 | tf_op jit(solution)/shard_map/ppermute | solution.py:19
  32.0 6.3 %copy-start.2 = (bf16[27,128,256]{2,1,0:T(8,128)(2,1)S(1)}, bf16[27,128,256]{2,1,0:T(8,128)(2,1)}, u32[]{:S(2)}) copy-start(bf16[27,128,256]{2,1,0:T(8,128)(2,1)} %param.11) | copy-start | bytes 5308420
  38.3 4.9 %copy-start.1 = (f32[27,128,256]{2,1,0:T(8,128)}, f32[27,128,256]{2,1,0:T(8,128)S(1)}, u32[]{:S(2)}) copy-start(f32[27,128,256]{2,1,0:T(8,128)S(1)} %fusion.12) | copy-start | bytes 10616836
  47.2 24.4 %collective-permute-start.3 = (bf16[128,1,1024]{0,2,1:T(8,128)(2,1)S(1)}, bf16[128,1,1024]{0,2,1:T(8,128)(2,1)S(1)}, u32[]{:S(2)}, u32[]{:S(2)}) collective-permute-start(bf16[128,1,1024]{0,2,1:T(8,128)(2,1)S(1)} %get-tuple-element.54), channel_id=1, source_target_pairs={{0,1},{1,2},{2,3},{3,4},{4,5},{5,6},{6,7},{7,8},{8,9},{9,10},{10,1... | collective-permute-start | bytes 786440 | tf_op jit(solution)/shard_map/ppermute | solution.py:19
  50.6 21.1 %collective-permute-start.2 = (bf16[128,1,1024]{0,2,1:T(8,128)(2,1)S(1)}, bf16[128,1,1024]{0,2,1:T(8,128)(2,1)S(1)}, u32[]{:S(2)}, u32[]{:S(2)}) collective-permute-start(bf16[128,1,1024]{0,2,1:T(8,128)(2,1)S(1)} %get-tuple-element.55), channel_id=1, source_target_pairs={{1,0},{2,1},{3,2},{4,3},{5,4},{6,5},{7,6},{8,7},{9,8},{10,9},{11,1... | collective-permute-start | bytes 786440 | tf_op jit(solution)/shard_map/ppermute | solution.py:21
  70.7 0.9 copy-start.3
  74.2 3.7 %copy-start.4 = (bf16[27,64,128]{2,1,0:T(8,128)(2,1)S(1)}, bf16[27,64,128]{2,1,0:T(8,128)(2,1)}, u32[]{:S(2)}) copy-start(bf16[27,64,128]{2,1,0:T(8,128)(2,1)} %param.10) | copy-start | bytes 1327108
Sparse Core Ops, SparseCore 0:
  71.8 162.8 all-reduce.14
where the time goes:
time: 248 us
  waiting for transfers between devices  148 us (60%)
  matrix products  29.7 us (12%)
  other arithmetic  27.2 us (11%)
  starting transfers between devices  21.9 us (9%)
  between operations  15.2 us (6%)
  local copies, waits for them, and re-layouts  6.3 us (3%)
    psum x1, waiting for transfers between devices, per_device(): total_a, total_b = lax.psum((sums_a, sums_b), ('dp', 'space'))  148 us
    select_n x8, other arithmetic, window(): piece = jnp.where(inside, piece, jnp.zeros_like(piece))  18.8 us
    ppermute x4, starting transfers between devices, padded_2(): lax.ppermute(tail, axis, [(i, (i + 1) % count) for i in range(ends)])  16.5 us
    dot_general x54, matrix products, outer_product(): lax.dot_general(left, right, (((1,), (1,)), ((), ())), preferred_element_...  13.6 us
    dot_general x27, matrix products, per_device(): jnp.dot(weight_b[tap], mirror, preferred_element_type=jnp.float32)  8.12 us
    dot_general x27, matrix products, per_device(): jnp.dot(weight_a[tap], mirror, preferred_element_type=jnp.float32)  8 us
    mul x2, other arithmetic, per_device(): return (input_grad, total_a * scale_a, total_b * scale_b)  6.44 us
    ppermute x4, starting transfers between devices, padded_2(): lax.ppermute(head, axis, [((i + 1) % count, i) for i in range(ends)])  5.34 us
  transfers between devices with their start and end apart: 9, of which 1 were waited for; matrix products, arithmetic and copies ran while one was open for 22% of the time, Pallas kernels for 0%

commit v1 on v0

--- a/solution.py
+++ b/solution.py
@@ -4,6 +4,8 @@
 import jax.numpy as jnp
 from jax import lax
 from jax.sharding import PartitionSpec as P
+from jax.experimental import pallas as pl
+from jax.experimental.pallas import tpu as pltpu
 
 negative_slope = 0.3
 
@@ -45,6 +47,110 @@
     return lax.dot_general(
         left, right, (((1,), (1,)), ((), ())), preferred_element_type=jnp.float32
     )
+
+
+def _all_reduce_kernel(x_ref, o_ref, full, recv_a, acc_a, recv_b, acc_b, recv_c, acc_c, recv_d, sends, recvs):
+    rows = x_ref.shape[0]
+    half, eighth, piece = rows // 2, rows // 8, rows // 32
+    mesh_id = pl.DeviceIdType.MESH
+    dp = lax.axis_index("dp")
+    sp = lax.axis_index("space")
+    core, xi, yi, zi = dp % 2, dp // 2, sp // 4, sp % 4
+    partner = (xi * 2 + (1 - core), sp)
+
+    def x_peer(k):
+        return (((xi + k) % 4) * 2 + core, sp)
+
+    def y_peer(k):
+        return (dp, ((yi + k) % 4) * 4 + zi)
+
+    def z_peer(k):
+        return (dp, yi * 4 + (zi + k) % 4)
+
+    peers = [partner] + [f(k) for f in (x_peer, y_peer, z_peer) for k in (1, 2, 3)]
+    barrier = pltpu.get_barrier_semaphore()
+    for peer in peers:
+        pl.semaphore_signal(barrier, inc=1, device_id=peer, device_id_type=mesh_id)
+    pl.semaphore_wait(barrier, len(peers))
+
+    def rows_at(start, size):
+        return pl.ds(pl.multiple_of(start, 8), size)
+
+    def exchange(pairs, first):
+        copies = []
+        for n, (src, dst, peer) in enumerate(pairs):
+            copy = pltpu.make_async_remote_copy(
+                src_ref=src,
+                dst_ref=dst,
+                send_sem=sends.at[first + n],
+                recv_sem=recvs.at[first + n],
+                device_id=peer,
+                device_id_type=mesh_id,
+            )
+            copy.start()
+            copies.append(copy)
+        for copy in copies:
+            copy.wait()
+
+    exchange([(x_ref.at[rows_at((1 - core) * half, half)], recv_a, partner)], 0)
+    acc_a[...] = x_ref[rows_at(core * half, half), :] + recv_a[...]
+    exchange(
+        [(acc_a.at[rows_at(((xi + k) % 4) * eighth, eighth)], recv_b.at[k - 1], x_peer(k)) for k in (1, 2, 3)], 1
+    )
+    acc_b[...] = acc_a[rows_at(xi * eighth, eighth), :] + recv_b[0] + recv_b[1] + recv_b[2]
+    exchange(
+        [(acc_b.at[rows_at(((yi + k) % 4) * piece, piece)], recv_c.at[k - 1], y_peer(k)) for k in (1, 2, 3)], 4
+    )
+    acc_c[...] = acc_b[rows_at(yi * piece, piece), :] + recv_c[0] + recv_c[1] + recv_c[2]
+    recv_d[0] = acc_c[...]
+    exchange([(acc_c, recv_d.at[k], z_peer(k)) for k in (1, 2, 3)], 7)
+    total = recv_d[zi % 4]
+    for j in (1, 2, 3):
+        total = total + recv_d[(zi - j + 4) % 4]
+    own = core * half + xi * eighth + yi * piece
+    full[rows_at(own, piece), :] = total
+    block = full.at[rows_at(own, piece)]
+    exchange([(block, block, y_peer(k)) for k in (1, 2, 3)], 10)
+    block = full.at[rows_at(core * half + xi * eighth, eighth)]
+    exchange([(block, block, x_peer(k)) for k in (1, 2, 3)], 13)
+    block = full.at[rows_at(core * half, half)]
+    exchange([(block, block, partner)], 16)
+    o_ref[...] = full[...]
+
+
+def all_reduce(parts):
+    flat = jnp.concatenate([p.reshape(-1) for p in parts])
+    count = flat.shape[0]
+    unit = 128 * 256
+    rows = -(-count // unit) * 256
+    flat = jnp.pad(flat, (0, rows * 128 - count)).reshape(rows, 128)
+    half, eighth, piece = rows // 2, rows // 8, rows // 32
+    f32 = jnp.float32
+    summed = pl.pallas_call(
+        _all_reduce_kernel,
+        out_shape=jax.ShapeDtypeStruct((rows, 128), f32),
+        in_specs=[pl.BlockSpec(memory_space=pltpu.VMEM)],
+        out_specs=pl.BlockSpec(memory_space=pltpu.VMEM),
+        scratch_shapes=[
+            pltpu.VMEM((rows, 128), f32),
+            pltpu.VMEM((half, 128), f32),
+            pltpu.VMEM((half, 128), f32),
+            pltpu.VMEM((3, eighth, 128), f32),
+            pltpu.VMEM((eighth, 128), f32),
+            pltpu.VMEM((3, piece, 128), f32),
+            pltpu.VMEM((piece, 128), f32),
+            pltpu.VMEM((4, piece, 128), f32),
+            pltpu.SemaphoreType.DMA((17,)),
+            pltpu.SemaphoreType.DMA((17,)),
+        ],
+        compiler_params=pltpu.CompilerParams(collective_id=0, has_side_effects=True),
+    )(flat)
+    summed = summed.reshape(-1)
+    out, start = [], 0
+    for p in parts:
+        out.append(summed[start : start + p.size].reshape(p.shape))
+        start += p.size
+    return out
 
 
 def per_device(layer_input, hidden_pre, output_pre, output_grad, weight_a, weight_b):
@@ -104,7 +210,7 @@
         )
     sums_a = jnp.stack(terms_a)
     input_grad = back_a.astype(jnp.bfloat16).reshape(1, chan_in, depth_a, side * side)
-    total_a, total_b = lax.psum((sums_a, sums_b), ("dp", "space"))
+    total_a, total_b = all_reduce((sums_a, sums_b))
     samples = lax.axis_size("dp")
     planes_a = depth_a * lax.axis_size("space")
     scale_a = 1.0 / math.sqrt(samples * planes_a * side * side)

time: 248 us -> 196 us (0.79)
  waiting for transfers between devices: 148 us -> 0.02 us
  Pallas kernels: 0 us -> 99.4 us
  between operations: 15.2 us -> 1.67 us
  local copies, waits for them, and re-layouts: 6.3 us -> 10 us
  other arithmetic: 27.2 us -> 30.9 us
    psum x1 -> x0, waiting for transfers between devices: 148 us -> none  [per_device(): total_a, total_b = lax.psum((sums_a, sums_b), ('dp', 'space'))]
    pallas_call x0 -> x1, Pallas kernels: none -> 99.4 us  [all_reduce(): pl.pallas_call(_all_reduce_kernel, out_shape=jax.ShapeDtypeStruct((rows,...]
    reshape x0 -> x1, other arithmetic: none -> 3.04 us  [all_reduce(): flat = jnp.pad(flat, (0, rows * 128 - count)).reshape(rows, 128)]
    mul x0 -> x1, local copies, waits for them, and re-layouts: none -> 2.7 us  [per_device(): return (input_grad, total_a * scale_a, total_b * scale_b)]
    select_n x8, other arithmetic: 18.8 us -> 21.5 us  [window(): piece = jnp.where(inside, piece, jnp.zeros_like(piece))]
  transfers between devices with their start and end apart: 9 -> 8, of which waited for: 1 -> 0; matrix products, arithmetic and copies ran while one was open for 22% -> 27% of each run, Pallas kernels for 0% -> 51%
where the time goes in v1:
time: 196 us; the launch traced here: 195 us
  Pallas kernels  99.4 us (51%)
  other arithmetic  30.9 us (16%)
  matrix products  30.1 us (15%)
  starting transfers between devices  22.8 us (12%)
  local copies, waits for them, and re-layouts  10 us (5%)
    pallas_call x1, Pallas kernels, all_reduce(): pl.pallas_call(_all_reduce_kernel, out_shape=jax.ShapeDtypeStruct((rows,...  99.4 us
    select_n x8, other arithmetic, window(): piece = jnp.where(inside, piece, jnp.zeros_like(piece))  21.5 us
    ppermute x4, starting transfers between devices, padded_2(): lax.ppermute(tail, axis, [(i, (i + 1) % count) for i in range(ends)])  17.4 us
    dot_general x54, matrix products, outer_product(): lax.dot_general(left, right, (((1,), (1,)), ((), ())), preferred_element_...  14 us
    dot_general x27, matrix products, per_device(): jnp.dot(weight_b[tap], mirror, preferred_element_type=jnp.float32)  8.12 us
    dot_general x27, matrix products, per_device(): jnp.dot(weight_a[tap], mirror, preferred_element_type=jnp.float32)  8.08 us
    ppermute x4, starting transfers between devices, padded_2(): lax.ppermute(head, axis, [((i + 1) % count, i) for i in range(ends)])  5.38 us
    unnamed x39, local copies, waits for them, and re-layouts  4.62 us
  transfers between devices with their start and end apart: 8, of which 0 were waited for; matrix products, arithmetic and copies ran while one was open for 27% of the time, Pallas kernels for 51%

profile of v1, /device:TPU:1, one launch (start us, length us, event | category | flops | bytes accessed | tf_op | source)
XLA Modules:
  0.0 194.9 jit_solution(11466925381419236752)
XLA Ops:
  0.6 1.1 multiply_convert_fusion.1
  1.7 4.4 %collective-permute-start.1 = (bf16[256,1,256]{2,0,1:T(8,128)(2,1)S(1)}, bf16[256,1,256]{2,0,1:T(8,128)(2,1)S(1)}, u32[]{:S(2)}, u32[]{:S(2)}) collective-permute-start(bf16[256,1,256]{2,0,1:T(8,128)(2,1)S(1)} %bitcast.924), channel_id=1, source_target_pairs={{0,1},{1,2},{2,3},{3,4},{4,5},{5,6},{6,7},{7,8},{8,9},{9,10},{10,1... | collective-permute-start | bytes 393224 | tf_op jit(solution)/shard_map/ppermute | solution.py:21
  6.1 1.3 collective-permute-start
  7.4 1.4 copy.37
  9.0 0.4 reduce_sum.18
  9.4 4.2 %collective-permute-start.6 = (bf16[128,1,256]{0,2,1:T(8,128)(2,1)S(1)}, bf16[128,1,256]{0,2,1:T(8,128)(2,1)S(1)}, u32[]{:S(2)}, u32[]{:S(2)}) collective-permute-start(bf16[128,1,256]{0,2,1:T(8,128)(2,1)S(1)} %bitcast.935), channel_id=1, source_target_pairs={{0,1},{1,2},{2,3},{3,4},{4,5},{5,6},{6,7},{7,8},{8,9},{9,10},{10,1... | collective-permute-start | bytes 196616 | tf_op jit(solution)/shard_map/ppermute | solution.py:21
  13.6 1.3 collective-permute-start.7
  14.9 0.4 fusion.579
  15.3 1.3 collective-permute-start.5
  16.9 1.3 broadcast_select_fusion.7
  18.6 4.8 %collective-permute-start.4 = (bf16[64,1,1024]{2,1,0:T(2,128)(2,1)S(1)}, bf16[64,1,1024]{2,1,0:T(2,128)(2,1)S(1)}, u32[]{:S(2)}, u32[]{:S(2)}) collective-permute-start(bf16[64,1,1024]{2,1,0:T(2,128)(2,1)S(1)} %get-tuple-element.94), channel_id=1, source_target_pairs={{0,1},{1,2},{2,3},{3,4},{4,5},{5,6},{6,7},{7,8},{8,9},{9,10},{10,1... | collective-permute-start | bytes 393224 | tf_op jit(solution)/shard_map/ppermute | solution.py:21
  31.2 1.8 copy.92
  33.3 0.3 fusion.87
  33.7 0.3 convolution_add_fusion.30
  34.0 0.3 convolution_add_fusion.29
  34.3 0.3 convolution_add_fusion.28
  34.9 0.3 convolution_add_fusion.26
  35.2 0.3 convolution_add_fusion.25
  35.5 0.3 convolution_add_fusion.24
  35.8 0.3 convolution_add_fusion.23
  36.1 0.3 convolution_add_fusion.22
  36.4 0.3 convolution_add_fusion.21
  36.8 0.3 convolution_add_fusion.20
  37.3 0.3 convolution_add_fusion.18
  37.6 0.3 convolution_add_fusion.17
  37.9 0.3 fusion.49
  38.2 0.3 fusion.48
  38.6 0.3 convolution_bitcast_fusion.40
  38.9 0.3 fusion.47
  39.2 0.3 fusion.46
  39.5 0.3 fusion.45
  39.8 0.3 fusion.44
  40.4 0.3 fusion.42
  40.7 0.3 fusion.41
  41.0 0.3 fusion.52
  41.9 0.9 fusion.578
  42.8 4.0 %collective-permute-start.3 = (bf16[128,1,1024]{0,2,1:T(8,128)(2,1)}, bf16[128,1,1024]{0,2,1:T(8,128)(2,1)}, u32[]{:S(2)}, u32[]{:S(2)}) collective-permute-start(bf16[128,1,1024]{0,2,1:T(8,128)(2,1)} %get-tuple-element.52), channel_id=1, source_target_pairs={{0,1},{1,2},{2,3},{3,4},{4,5},{5,6},{6,7},{7,8},{8,9},{9,10},{10,1... | collective-permute-start | bytes 786440 | tf_op jit(solution)/shard_map/ppermute | solution.py:21
  46.8 1.5 collective-permute-start.2
  48.3 3.4 %broadcast_select_fusion.14 = (bf16[64,2,1024]{2,1,0:T(2,128)(2,1)S(1)}, bf16[64,2,1024]{2,1,0:T(2,128)(2,1)S(1)}, bf16[64,2,1024]{2,1,0:T(2,128)(2,1)S(1)}, bf1...) fusion(pred[1024]{0:T(1024)(128)(4,1)S(1)} %fusion.522, ...), kind=kLoop, calls=%fused_computation.235 | loop fusion | flops 1966080 | bytes 2885632 | tf_op jit(solution)/shard_map/jit(_where)/select_n | solution.py:42
  51.7 2.9 %broadcast_select_fusion.10 = (bf16[64,2,1024]{2,1,0:T(2,128)(2,1)S(1)}, bf16[64,2,1024]{2,1,0:T(2,128)(2,1)S(1)}, bf16[64,2,1024]{2,1,0:T(2,128)(2,1)S(1)}, bf1...) fusion(pred[1024]{0:T(1024)(128)(4,1)S(1)} %get-tuple-element.1, ...), kind=kLoop, calls=%fused_computation.231 | loop fusion | flops 1048576 | bytes 2362368 | tf_op jit(solution)/shard_map/jit(_where)/select_n | solution.py:42
  55.4 2.9 %broadcast_select_fusion.4 = (bf16[64,2,1024]{2,1,0:T(2,128)(2,1)S(1)}, bf16[64,2,1024]{2,1,0:T(2,128)(2,1)S(1)}, bf16[64,2,1024]{2,1,0:T(2,128)(2,1)S(1)}, bf16...) fusion(pred[1024]{0:T(1024)(128)(4,1)S(1)} %get-tuple-element.1, ...), kind=kLoop, calls=%fused_computation.225 | loop fusion | flops 1048576 | bytes 2362368 | tf_op jit(solution)/shard_map/jit(_where)/select_n | solution.py:42
  58.9 2.1 %broadcast_select_fusion = (bf16[128,2,32,16,2]{0,4,3,2,1:T(2,128)(2,1)}, bf16[128,2,32,16,2]{0,4,3,2,1:T(2,128)(2,1)S(1)}) fusion(pred[32,16,2]{2,1,0:T(8,128)(4,1)S(1)} %copy.38, f32[128,2,32,16,2]{0,4,3,2,1:T(2,128)S(1)} %bitcast.949, f32[128,32,16]{0,2,1:T(8,128)S(1)} %bitcast.952), kind=kLoop, calls=%fused_computation.194 | loop fusion | flops 786432 | bytes 2360320 | tf_op jit(solution)/shard_map/jit(_where)/select_n | solution.py:42
  67.4 3.0 %fusion.x_ref = f32[8704,128]{1,0:T(8,128)} fusion(f32[884736]{0:T(1024)S(1)} %bitcast.934, f32[221184]{0:T(1024)S(1)} %bitcast.1036), kind=kLoop, calls=%fused_computation.1 | loop fusion | flops 4456448 | bytes 8880128 | tf_op jit(solution)/shard_map/reshape | solution.py:126
  70.4 99.4 %shard_map.85 = f32[8704,128]{1,0:T(8,128)} custom-call(f32[8704,128]{1,0:T(8,128)} %fusion.x_ref), custom_call_target="tpu_custom_call" | custom-call | tf_op jit(solution)/shard_map/pallas_call | solution.py:129
  169.8 2.3 %slice_multiply_fusion = f32[6912,128]{1,0:T(8,128)S(1)} fusion(f32[8704,128]{1,0:T(8,128)} %shard_map.85), kind=kLoop, calls=%fused_computation.3 | loop fusion | flops 884736 | bytes 7077888 | tf_op jit(solution)/shard_map/mul | solution.py:218
  172.1 2.7 %mul.341 = f32[27,128,256]{2,1,0:T(8,128)} reshape(f32[6912,128]{1,0:T(8,128)S(1)} %slice_multiply_fusion) | data formatting | bytes 7077888 | tf_op jit(solution)/shard_map/mul | solution.py:218
  174.8 2.1 %slice_multiply_fusion.1 = f32[1728,128]{1,0:T(8,128)} fusion(f32[8704,128]{1,0:T(8,128)} %shard_map.85), kind=kLoop, calls=%fused_computation.195 | loop fusion | flops 221184 | bytes 1769472 | tf_op jit(solution)/shard_map/mul | solution.py:218
  177.0 5.3 %broadcast_select_fusion.1 = (bf16[128,2,1024]{0,2,1:T(8,128)(2,1)S(1)}, bf16[128,2,1024]{0,2,1:T(8,128)(2,1)S(1)}, bf16[128,2,1024]{0,2,1:T(8,128)(2,1)S(1)}, b...) fusion(pred[1024]{0:T(1024)(128)(4,1)S(1)} %fusion.522, ...), kind=kLoop, calls=%fused_computation.222 | loop fusion | flops 4718592 | bytes 7343104 | tf_op jit(solution)/shard_map/jit(_where)/select_n | solution.py:42
  182.3 3.5 %slice_select_fusion.16 = (bf16[128,2,1024]{0,2,1:T(8,128)(2,1)S(1)}, bf16[128,2,1024]{0,2,1:T(8,128)(2,1)S(1)}, bf16[128,2,1024]{0,2,1:T(8,128)(2,1)S(1)}, bf16...) fusion(pred[1024]{0:T(1024)(128)(4,1)S(1)} %get-tuple-element.1, ...), kind=kLoop, calls=%fused_computation.214 | loop fusion | flops 4194304 | bytes 9440256 | tf_op jit(solution)/shard_map/jit(_where)/select_n | solution.py:42
  186.1 0.3 convolution_add_fusion.15
  188.2 0.3 convolution_add_fusion.8
  189.2 0.3 convolution_add_fusion.5
  189.5 0.3 convolution_add_fusion.4
  190.4 0.3 convolution_add_fusion.1
  190.7 0.3 fusion.11
  191.0 0.3 fusion.10
  191.3 0.3 fusion.9
  191.6 0.3 fusion.8
  191.9 0.3 fusion.7
  192.2 0.3 fusion.6
  192.5 0.3 fusion.5
  192.8 0.3 fusion.4
  193.7 0.3 fusion.12
  194.0 0.9 reshape.946
  (129 shorter events, 21.5 us)
Async XLA Ops:
  0.6 14.3 %copy-start = (bf16[1,64,2,1024]{3,2,1,0:T(2,128)(2,1)S(1)}, bf16[1,64,2,1024]{3,2,1,0:T(2,128)(2,1)}, u32[]{:S(2)}) copy-start(bf16[1,64,2,1024]{3,2,1,0:T(2,128)(2,1)} %param.6) | copy-start | bytes 786436
  1.7 36.9 %collective-permute-start.1 = (bf16[256,1,256]{2,0,1:T(8,128)(2,1)S(1)}, bf16[256,1,256]{2,0,1:T(8,128)(2,1)S(1)}, u32[]{:S(2)}, u32[]{:S(2)}) collective-permute-start(bf16[256,1,256]{2,0,1:T(8,128)(2,1)S(1)} %bitcast.924), channel_id=1, source_target_pairs={{0,1},{1,2},{2,3},{3,4},{4,5},{5,6},{6,7},{7,8},{8,9},{9,10},{10,1... | collective-permute-start | bytes 393224 | tf_op jit(solution)/shard_map/ppermute | solution.py:21
  6.1 26.9 %collective-permute-start = (bf16[256,1,256]{2,0,1:T(8,128)(2,1)S(1)}, bf16[256,1,256]{2,0,1:T(8,128)(2,1)S(1)}, u32[]{:S(2)}, u32[]{:S(2)}) collective-permute-start(bf16[256,1,256]{2,0,1:T(8,128)(2,1)S(1)} %bitcast.925), channel_id=1, source_target_pairs={{1,0},{2,1},{3,2},{4,3},{5,4},{6,5},{7,6},{8,7},{9,8},{10,9},{11,1... | collective-permute-start | bytes 393224 | tf_op jit(solution)/shard_map/ppermute | solution.py:23
  9.4 9.2 %collective-permute-start.6 = (bf16[128,1,256]{0,2,1:T(8,128)(2,1)S(1)}, bf16[128,1,256]{0,2,1:T(8,128)(2,1)S(1)}, u32[]{:S(2)}, u32[]{:S(2)}) collective-permute-start(bf16[128,1,256]{0,2,1:T(8,128)(2,1)S(1)} %bitcast.935), channel_id=1, source_target_pairs={{0,1},{1,2},{2,3},{3,4},{4,5},{5,6},{6,7},{7,8},{8,9},{9,10},{10,1... | collective-permute-start | bytes 196616 | tf_op jit(solution)/shard_map/ppermute | solution.py:21
  13.6 15.0 %collective-permute-start.7 = (bf16[128,1,256]{0,2,1:T(8,128)(2,1)S(1)}, bf16[128,1,256]{0,2,1:T(8,128)(2,1)S(1)}, u32[]{:S(2)}, u32[]{:S(2)}) collective-permute-start(bf16[128,1,256]{0,2,1:T(8,128)(2,1)S(1)} %bitcast.936), channel_id=1, source_target_pairs={{1,0},{2,1},{3,2},{4,3},{5,4},{6,5},{7,6},{8,7},{9,8},{10,9},{11,1... | collective-permute-start | bytes 196616 | tf_op jit(solution)/shard_map/ppermute | solution.py:23
  15.3 33.1 %collective-permute-start.5 = (bf16[64,1,1024]{2,1,0:T(2,128)(2,1)S(1)}, bf16[64,1,1024]{2,1,0:T(2,128)(2,1)S(1)}, u32[]{:S(2)}, u32[]{:S(2)}) collective-permute-start(bf16[64,1,1024]{2,1,0:T(2,128)(2,1)S(1)} %get-tuple-element.93), channel_id=1, source_target_pairs={{1,0},{2,1},{3,2},{4,3},{5,4},{6,5},{7,6},{8,7},{9,8},{10,9},{11,1... | collective-permute-start | bytes 393224 | tf_op jit(solution)/shard_map/ppermute | solution.py:23
  18.6 29.7 %collective-permute-start.4 = (bf16[64,1,1024]{2,1,0:T(2,128)(2,1)S(1)}, bf16[64,1,1024]{2,1,0:T(2,128)(2,1)S(1)}, u32[]{:S(2)}, u32[]{:S(2)}) collective-permute-start(bf16[64,1,1024]{2,1,0:T(2,128)(2,1)S(1)} %get-tuple-element.94), channel_id=1, source_target_pairs={{0,1},{1,2},{2,3},{3,4},{4,5},{5,6},{6,7},{7,8},{8,9},{9,10},{10,1... | collective-permute-start | bytes 393224 | tf_op jit(solution)/shard_map/ppermute | solution.py:21
  31.2 1.9 copy-start.3
  41.8 12.8 %copy-start.1 = (bf16[128,2,1024]{0,2,1:T(8,128)(2,1)}, bf16[128,2,1024]{0,2,1:T(8,128)(2,1)S(1)}, u32[]{:S(2)}) copy-start(bf16[128,2,1024]{0,2,1:T(8,128)(2,1)S(1)} %fusion.81) | copy-start | bytes 1572868
  42.8 134.2 %collective-permute-start.3 = (bf16[128,1,1024]{0,2,1:T(8,128)(2,1)}, bf16[128,1,1024]{0,2,1:T(8,128)(2,1)}, u32[]{:S(2)}, u32[]{:S(2)}) collective-permute-start(bf16[128,1,1024]{0,2,1:T(8,128)(2,1)} %get-tuple-element.52), channel_id=1, source_target_pairs={{0,1},{1,2},{2,3},{3,4},{4,5},{5,6},{6,7},{7,8},{8,9},{9,10},{10,1... | collective-permute-start | bytes 786440 | tf_op jit(solution)/shard_map/ppermute | solution.py:21
  46.8 130.2 %collective-permute-start.2 = (bf16[128,1,1024]{0,2,1:T(8,128)(2,1)}, bf16[128,1,1024]{0,2,1:T(8,128)(2,1)}, u32[]{:S(2)}, u32[]{:S(2)}) collective-permute-start(bf16[128,1,1024]{0,2,1:T(8,128)(2,1)} %get-tuple-element.53), channel_id=1, source_target_pairs={{1,0},{2,1},{3,2},{4,3},{5,4},{6,5},{7,6},{8,7},{9,8},{10,9},{11,1... | collective-permute-start | bytes 786440 | tf_op jit(solution)/shard_map/ppermute | solution.py:23
  182.3 3.5 %copy-start.4 = (bf16[27,64,128]{2,1,0:T(8,128)(2,1)S(1)}, bf16[27,64,128]{2,1,0:T(8,128)(2,1)}, u32[]{:S(2)}) copy-start(bf16[27,64,128]{2,1,0:T(8,128)(2,1)} %param.10) | copy-start | bytes 1327108
  188.5 1.2 copy-start.2

commit v2 on v1

--- a/solution.py
+++ b/solution.py
@@ -49,82 +49,99 @@
     )
 
 
-def _all_reduce_kernel(x_ref, o_ref, full, recv_a, acc_a, recv_b, acc_b, recv_c, acc_c, recv_d, sends, recvs):
+def _all_reduce_kernel(x_ref, o_ref, full, recv_a, acc_a, recv_1, acc_1, recv_2, acc_2, recv_3, sends, recvs):
     rows = x_ref.shape[0]
-    half, eighth, piece = rows // 2, rows // 8, rows // 32
+    half = rows // 2
+    part = half // 3
+    quarter, piece = part // 4, part // 16
     mesh_id = pl.DeviceIdType.MESH
     dp = lax.axis_index("dp")
     sp = lax.axis_index("space")
-    core, xi, yi, zi = dp % 2, dp // 2, sp // 4, sp % 4
-    partner = (xi * 2 + (1 - core), sp)
-
-    def x_peer(k):
-        return (((xi + k) % 4) * 2 + core, sp)
-
-    def y_peer(k):
-        return (dp, ((yi + k) % 4) * 4 + zi)
-
-    def z_peer(k):
-        return (dp, yi * 4 + (zi + k) % 4)
-
-    peers = [partner] + [f(k) for f in (x_peer, y_peer, z_peer) for k in (1, 2, 3)]
+    core = dp % 2
+    spot = {"x": dp // 2, "y": sp // 4, "z": sp % 4}
+    partner = (spot["x"] * 2 + (1 - core), sp)
+
+    def peer(axis, k):
+        moved = dict(spot)
+        moved[axis] = (spot[axis] + k) % 4
+        return (moved["x"] * 2 + core, moved["y"] * 4 + moved["z"])
+
+    orders = (("x", "y", "z"), ("y", "z", "x"), ("z", "x", "y"))
+    peers = [partner] + [peer(axis, k) for axis in "xyz" for k in (1, 2, 3)]
     barrier = pltpu.get_barrier_semaphore()
-    for peer in peers:
-        pl.semaphore_signal(barrier, inc=1, device_id=peer, device_id_type=mesh_id)
+    for other in peers:
+        pl.semaphore_signal(barrier, inc=1, device_id=other, device_id_type=mesh_id)
     pl.semaphore_wait(barrier, len(peers))
 
     def rows_at(start, size):
         return pl.ds(pl.multiple_of(start, 8), size)
 
-    def exchange(pairs, first):
+    used = [0]
+
+    def exchange(triples):
         copies = []
-        for n, (src, dst, peer) in enumerate(pairs):
+        for src, dst, other in triples:
             copy = pltpu.make_async_remote_copy(
                 src_ref=src,
                 dst_ref=dst,
-                send_sem=sends.at[first + n],
-                recv_sem=recvs.at[first + n],
-                device_id=peer,
+                send_sem=sends.at[used[0]],
+                recv_sem=recvs.at[used[0]],
+                device_id=other,
                 device_id_type=mesh_id,
             )
+            used[0] += 1
             copy.start()
             copies.append(copy)
         for copy in copies:
             copy.wait()
 
-    exchange([(x_ref.at[rows_at((1 - core) * half, half)], recv_a, partner)], 0)
+    exchange([(x_ref.at[rows_at((1 - core) * half, half)], recv_a, partner)])
     acc_a[...] = x_ref[rows_at(core * half, half), :] + recv_a[...]
-    exchange(
-        [(acc_a.at[rows_at(((xi + k) % 4) * eighth, eighth)], recv_b.at[k - 1], x_peer(k)) for k in (1, 2, 3)], 1
-    )
-    acc_b[...] = acc_a[rows_at(xi * eighth, eighth), :] + recv_b[0] + recv_b[1] + recv_b[2]
-    exchange(
-        [(acc_b.at[rows_at(((yi + k) % 4) * piece, piece)], recv_c.at[k - 1], y_peer(k)) for k in (1, 2, 3)], 4
-    )
-    acc_c[...] = acc_b[rows_at(yi * piece, piece), :] + recv_c[0] + recv_c[1] + recv_c[2]
-    recv_d[0] = acc_c[...]
-    exchange([(acc_c, recv_d.at[k], z_peer(k)) for k in (1, 2, 3)], 7)
-    total = recv_d[zi % 4]
-    for j in (1, 2, 3):
-        total = total + recv_d[(zi - j + 4) % 4]
-    own = core * half + xi * eighth + yi * piece
-    full[rows_at(own, piece), :] = total
-    block = full.at[rows_at(own, piece)]
-    exchange([(block, block, y_peer(k)) for k in (1, 2, 3)], 10)
-    block = full.at[rows_at(core * half + xi * eighth, eighth)]
-    exchange([(block, block, x_peer(k)) for k in (1, 2, 3)], 13)
+    triples = []
+    for p, order in enumerate(orders):
+        for k in (1, 2, 3):
+            block = p * part + ((spot[order[0]] + k) % 4) * quarter
+            triples.append((acc_a.at[rows_at(block, quarter)], recv_1.at[p, k - 1], peer(order[0], k)))
+    exchange(triples)
+    for p, order in enumerate(orders):
+        mine = p * part + spot[order[0]] * quarter
+        acc_1[p] = acc_a[rows_at(mine, quarter), :] + recv_1[p, 0] + recv_1[p, 1] + recv_1[p, 2]
+    triples = []
+    for p, order in enumerate(orders):
+        for k in (1, 2, 3):
+            block = ((spot[order[1]] + k) % 4) * piece
+            triples.append((acc_1.at[p, rows_at(block, piece)], recv_2.at[p, k - 1], peer(order[1], k)))
+    exchange(triples)
+    for p, order in enumerate(orders):
+        mine = spot[order[1]] * piece
+        recv_3[p, 0] = acc_1[p, rows_at(mine, piece), :] + recv_2[p, 0] + recv_2[p, 1] + recv_2[p, 2]
+    exchange([(recv_3.at[p, 0], recv_3.at[p, k], peer(order[2], k)) for p, order in enumerate(orders) for k in (1, 2, 3)])
+    spans = []
+    for p, order in enumerate(orders):
+        last = spot[order[2]]
+        total = recv_3[p, last % 4]
+        for j in (1, 2, 3):
+            total = total + recv_3[p, (last - j + 4) % 4]
+        outer = core * half + p * part + spot[order[0]] * quarter
+        own = outer + spot[order[1]] * piece
+        full[rows_at(own, piece), :] = total
+        spans.append((outer, own, order))
+    exchange([(full.at[rows_at(own, piece)], full.at[rows_at(own, piece)], peer(order[1], k)) for outer, own, order in spans for k in (1, 2, 3)])
+    exchange([(full.at[rows_at(outer, quarter)], full.at[rows_at(outer, quarter)], peer(order[0], k)) for outer, own, order in spans for k in (1, 2, 3)])
     block = full.at[rows_at(core * half, half)]
-    exchange([(block, block, partner)], 16)
+    exchange([(block, block, partner)])
     o_ref[...] = full[...]
 
 
 def all_reduce(parts):
     flat = jnp.concatenate([p.reshape(-1) for p in parts])
     count = flat.shape[0]
-    unit = 128 * 256
-    rows = -(-count // unit) * 256
+    unit = 128 * 6 * 16 * 8
+    rows = -(-count // unit) * 6 * 16 * 8
     flat = jnp.pad(flat, (0, rows * 128 - count)).reshape(rows, 128)
-    half, eighth, piece = rows // 2, rows // 8, rows // 32
+    half = rows // 2
+    part = half // 3
+    quarter, piece = part // 4, part // 16
     f32 = jnp.float32
     summed = pl.pallas_call(
         _all_reduce_kernel,
@@ -135,13 +152,13 @@
             pltpu.VMEM((rows, 128), f32),
             pltpu.VMEM((half, 128), f32),
             pltpu.VMEM((half, 128), f32),
-            pltpu.VMEM((3, eighth, 128), f32),
-            pltpu.VMEM((eighth, 128), f32),
+            pltpu.VMEM((3, 3, quarter, 128), f32),
+            pltpu.VMEM((3, quarter, 128), f32),
+            pltpu.VMEM((3, 3, piece, 128), f32),
             pltpu.VMEM((3, piece, 128), f32),
-            pltpu.VMEM((piece, 128), f32),
-            pltpu.VMEM((4, piece, 128), f32),
-            pltpu.SemaphoreType.DMA((17,)),
-            pltpu.SemaphoreType.DMA((17,)),
+            pltpu.VMEM((3, 4, piece, 128), f32),
+            pltpu.SemaphoreType.DMA((47,)),
+            pltpu.SemaphoreType.DMA((47,)),
         ],
         compiler_params=pltpu.CompilerParams(collective_id=0, has_side_effects=True),
     )(flat)

time: 196 us -> 158 us (0.81)
  Pallas kernels: 99.4 us -> 61.5 us
    pallas_call x1, Pallas kernels: 99.4 us -> 61.5 us  [all_reduce(): pl.pallas_call(_all_reduce_kernel, out_shape=jax.ShapeDtypeStruct((rows,...]
  transfers between devices with their start and end apart: 8 -> 8, of which waited for: 0 -> 0; matrix products, arithmetic and copies ran while one was open for 27% -> 33% of each run, Pallas kernels for 51% -> 39%
where the time goes in v2:
time: 158 us; the launch traced here: 157 us
  Pallas kernels  61.5 us (39%)
  other arithmetic  31.2 us (20%)
  matrix products  30.2 us (19%)
  starting transfers between devices  22.8 us (14%)
  local copies, waits for them, and re-layouts  10 us (6%)
  between operations  1.65 us (1%)
    pallas_call x1, Pallas kernels, all_reduce(): pl.pallas_call(_all_reduce_kernel, out_shape=jax.ShapeDtypeStruct((rows,...  61.5 us
    select_n x8, other arithmetic, window(): piece = jnp.where(inside, piece, jnp.zeros_like(piece))  21.6 us
    ppermute x4, starting transfers between devices, padded_2(): lax.ppermute(tail, axis, [(i, (i + 1) % count) for i in range(ends)])  17.4 us
    dot_general x54, matrix products, outer_product(): lax.dot_general(left, right, (((1,), (1,)), ((), ())), preferred_element_...  13.9 us
    dot_general x27, matrix products, per_device(): jnp.dot(weight_b[tap], mirror, preferred_element_type=jnp.float32)  8.12 us
    dot_general x27, matrix products, per_device(): jnp.dot(weight_a[tap], mirror, preferred_element_type=jnp.float32)  8.1 us
    ppermute x4, starting transfers between devices, padded_2(): lax.ppermute(head, axis, [((i + 1) % count, i) for i in range(ends)])  5.38 us
    unnamed x39, local copies, waits for them, and re-layouts  4.62 us
  transfers between devices with their start and end apart: 8, of which 0 were waited for; matrix products, arithmetic and copies ran while one was open for 33% of the time, Pallas kernels for 39%

profile of v2, /device:TPU:1, one launch (start us, length us, event | category | flops | bytes accessed | tf_op | source)
XLA Modules:
  0.0 157.3 jit_solution(8674851399810621028)
XLA Ops:
  0.6 1.1 multiply_convert_fusion.1
  1.7 4.4 %collective-permute-start.1 = (bf16[256,1,256]{2,0,1:T(8,128)(2,1)S(1)}, bf16[256,1,256]{2,0,1:T(8,128)(2,1)S(1)}, u32[]{:S(2)}, u32[]{:S(2)}) collective-permute-start(bf16[256,1,256]{2,0,1:T(8,128)(2,1)S(1)} %bitcast.924), channel_id=1, source_target_pairs={{0,1},{1,2},{2,3},{3,4},{4,5},{5,6},{6,7},{7,8},{8,9},{9,10},{10,1... | collective-permute-start | bytes 393224 | tf_op jit(solution)/shard_map/ppermute | solution.py:21
  6.1 1.3 collective-permute-start
  7.4 1.4 copy.37
  9.0 0.4 reduce_sum.18
  9.4 4.2 %collective-permute-start.6 = (bf16[128,1,256]{0,2,1:T(8,128)(2,1)S(1)}, bf16[128,1,256]{0,2,1:T(8,128)(2,1)S(1)}, u32[]{:S(2)}, u32[]{:S(2)}) collective-permute-start(bf16[128,1,256]{0,2,1:T(8,128)(2,1)S(1)} %bitcast.935), channel_id=1, source_target_pairs={{0,1},{1,2},{2,3},{3,4},{4,5},{5,6},{6,7},{7,8},{8,9},{9,10},{10,1... | collective-permute-start | bytes 196616 | tf_op jit(solution)/shard_map/ppermute | solution.py:21
  13.6 1.3 collective-permute-start.7
  14.9 0.4 fusion.579
  15.3 1.3 collective-permute-start.5
  16.9 1.3 broadcast_select_fusion.7
  18.6 4.8 %collective-permute-start.4 = (bf16[64,1,1024]{2,1,0:T(2,128)(2,1)S(1)}, bf16[64,1,1024]{2,1,0:T(2,128)(2,1)S(1)}, u32[]{:S(2)}, u32[]{:S(2)}) collective-permute-start(bf16[64,1,1024]{2,1,0:T(2,128)(2,1)S(1)} %get-tuple-element.94), channel_id=1, source_target_pairs={{0,1},{1,2},{2,3},{3,4},{4,5},{5,6},{6,7},{7,8},{8,9},{9,10},{10,1... | collective-permute-start | bytes 393224 | tf_op jit(solution)/shard_map/ppermute | solution.py:21
  31.2 1.8 %copy.92 = f32[432,2,8,128]{3,1,2,0:T(2,128)S(1)} copy(f32[432,2,8,128]{3,2,1,0:T(8,128)S(1)} %bitcast.950) | data formatting | bytes 7077888
  33.3 0.3 fusion.87
  33.7 0.3 convolution_add_fusion.30
  34.0 0.3 convolution_add_fusion.29
  34.3 0.3 convolution_add_fusion.28
  34.9 0.3 convolution_add_fusion.26
  35.2 0.3 convolution_add_fusion.25
  35.5 0.3 convolution_add_fusion.24
  35.8 0.3 convolution_add_fusion.23
  36.1 0.3 convolution_add_fusion.22
  36.4 0.3 convolution_add_fusion.21
  36.8 0.3 convolution_add_fusion.20
  37.3 0.3 convolution_add_fusion.18
  37.6 0.3 convolution_add_fusion.17
  37.9 0.3 fusion.49
  38.2 0.3 fusion.48
  38.6 0.3 convolution_bitcast_fusion.40
  38.9 0.3 fusion.47
  39.2 0.3 fusion.46
  39.5 0.3 fusion.45
  39.8 0.3 fusion.44
  40.4 0.3 fusion.42
  40.7 0.3 fusion.41
  41.0 0.3 fusion.52
  41.9 0.9 fusion.578
  42.8 4.1 %collective-permute-start.3 = (bf16[128,1,1024]{0,2,1:T(8,128)(2,1)}, bf16[128,1,1024]{0,2,1:T(8,128)(2,1)}, u32[]{:S(2)}, u32[]{:S(2)}) collective-permute-start(bf16[128,1,1024]{0,2,1:T(8,128)(2,1)} %get-tuple-element.52), channel_id=1, source_target_pairs={{0,1},{1,2},{2,3},{3,4},{4,5},{5,6},{6,7},{7,8},{8,9},{9,10},{10,1... | collective-permute-start | bytes 786440 | tf_op jit(solution)/shard_map/ppermute | solution.py:21
  46.8 1.5 collective-permute-start.2
  48.3 3.4 %broadcast_select_fusion.14 = (bf16[64,2,1024]{2,1,0:T(2,128)(2,1)S(1)}, bf16[64,2,1024]{2,1,0:T(2,128)(2,1)S(1)}, bf16[64,2,1024]{2,1,0:T(2,128)(2,1)S(1)}, bf1...) fusion(pred[1024]{0:T(1024)(128)(4,1)S(1)} %fusion.522, ...), kind=kLoop, calls=%fused_computation.235 | loop fusion | flops 1966080 | bytes 2885632 | tf_op jit(solution)/shard_map/jit(_where)/select_n | solution.py:42
  51.7 2.9 %broadcast_select_fusion.10 = (bf16[64,2,1024]{2,1,0:T(2,128)(2,1)S(1)}, bf16[64,2,1024]{2,1,0:T(2,128)(2,1)S(1)}, bf16[64,2,1024]{2,1,0:T(2,128)(2,1)S(1)}, bf1...) fusion(pred[1024]{0:T(1024)(128)(4,1)S(1)} %get-tuple-element.1, ...), kind=kLoop, calls=%fused_computation.231 | loop fusion | flops 1048576 | bytes 2362368 | tf_op jit(solution)/shard_map/jit(_where)/select_n | solution.py:42
  55.4 2.9 %broadcast_select_fusion.4 = (bf16[64,2,1024]{2,1,0:T(2,128)(2,1)S(1)}, bf16[64,2,1024]{2,1,0:T(2,128)(2,1)S(1)}, bf16[64,2,1024]{2,1,0:T(2,128)(2,1)S(1)}, bf16...) fusion(pred[1024]{0:T(1024)(128)(4,1)S(1)} %get-tuple-element.1, ...), kind=kLoop, calls=%fused_computation.225 | loop fusion | flops 1048576 | bytes 2362368 | tf_op jit(solution)/shard_map/jit(_where)/select_n | solution.py:42
  58.8 2.1 %broadcast_select_fusion = (bf16[128,2,32,16,2]{0,4,3,2,1:T(2,128)(2,1)}, bf16[128,2,32,16,2]{0,4,3,2,1:T(2,128)(2,1)S(1)}) fusion(pred[32,16,2]{2,1,0:T(8,128)(4,1)S(1)} %copy.38, f32[128,2,32,16,2]{0,4,3,2,1:T(2,128)S(1)} %bitcast.949, f32[128,32,16]{0,2,1:T(8,128)S(1)} %bitcast.952), kind=kLoop, calls=%fused_computation.194 | loop fusion | flops 786432 | bytes 2360320 | tf_op jit(solution)/shard_map/jit(_where)/select_n | solution.py:42
  67.4 3.2 %fusion.x_ref = f32[9216,128]{1,0:T(8,128)} fusion(f32[884736]{0:T(1024)S(1)} %bitcast.934, f32[221184]{0:T(1024)S(1)} %bitcast.1036), kind=kLoop, calls=%fused_computation.1 | loop fusion | flops 4718592 | bytes 9142272 | tf_op jit(solution)/shard_map/reshape | solution.py:141
  70.6 61.5 %shard_map.85 = f32[9216,128]{1,0:T(8,128)} custom-call(f32[9216,128]{1,0:T(8,128)} %fusion.x_ref), custom_call_target="tpu_custom_call" | custom-call | tf_op jit(solution)/shard_map/pallas_call | solution.py:146
  132.0 2.3 %slice_multiply_fusion = f32[6912,128]{1,0:T(8,128)S(1)} fusion(f32[9216,128]{1,0:T(8,128)} %shard_map.85), kind=kLoop, calls=%fused_computation.3 | loop fusion | flops 884736 | bytes 7077888 | tf_op jit(solution)/shard_map/mul | solution.py:235
  134.4 2.7 %mul.341 = f32[27,128,256]{2,1,0:T(8,128)} reshape(f32[6912,128]{1,0:T(8,128)S(1)} %slice_multiply_fusion) | data formatting | bytes 7077888 | tf_op jit(solution)/shard_map/mul | solution.py:235
  137.1 2.1 %slice_multiply_fusion.1 = f32[1728,128]{1,0:T(8,128)} fusion(f32[9216,128]{1,0:T(8,128)} %shard_map.85), kind=kLoop, calls=%fused_computation.195 | loop fusion | flops 221184 | bytes 1769472 | tf_op jit(solution)/shard_map/mul | solution.py:235
  139.2 5.5 %broadcast_select_fusion.1 = (bf16[128,2,1024]{0,2,1:T(8,128)(2,1)S(1)}, bf16[128,2,1024]{0,2,1:T(8,128)(2,1)S(1)}, bf16[128,2,1024]{0,2,1:T(8,128)(2,1)S(1)}, b...) fusion(pred[1024]{0:T(1024)(128)(4,1)S(1)} %fusion.522, ...), kind=kLoop, calls=%fused_computation.222 | loop fusion | flops 4718592 | bytes 7343104 | tf_op jit(solution)/shard_map/jit(_where)/select_n | solution.py:42
  144.7 3.5 %slice_select_fusion.16 = (bf16[128,2,1024]{0,2,1:T(8,128)(2,1)S(1)}, bf16[128,2,1024]{0,2,1:T(8,128)(2,1)S(1)}, bf16[128,2,1024]{0,2,1:T(8,128)(2,1)S(1)}, bf16...) fusion(pred[1024]{0:T(1024)(128)(4,1)S(1)} %get-tuple-element.1, ...), kind=kLoop, calls=%fused_computation.214 | loop fusion | flops 4194304 | bytes 9440256 | tf_op jit(solution)/shard_map/jit(_where)/select_n | solution.py:42
  148.5 0.3 convolution_add_fusion.15
  150.3 0.3 convolution_add_fusion.9
  150.6 0.3 convolution_add_fusion.8
  151.5 0.3 convolution_add_fusion.5
  151.8 0.3 convolution_add_fusion.4
  152.8 0.3 convolution_add_fusion.1
  153.1 0.3 fusion.11
  153.4 0.3 fusion.10
  153.7 0.3 fusion.9
  154.0 0.3 fusion.8
  154.3 0.3 fusion.7
  154.6 0.3 fusion.6
  154.9 0.3 fusion.5
  156.1 0.3 fusion.12
  156.4 0.9 reshape.946
  (129 shorter events, 21.5 us)
Async XLA Ops:
  0.6 14.3 %copy-start = (bf16[1,64,2,1024]{3,2,1,0:T(2,128)(2,1)S(1)}, bf16[1,64,2,1024]{3,2,1,0:T(2,128)(2,1)}, u32[]{:S(2)}) copy-start(bf16[1,64,2,1024]{3,2,1,0:T(2,128)(2,1)} %param.6) | copy-start | bytes 786436
  1.7 36.9 %collective-permute-start.1 = (bf16[256,1,256]{2,0,1:T(8,128)(2,1)S(1)}, bf16[256,1,256]{2,0,1:T(8,128)(2,1)S(1)}, u32[]{:S(2)}, u32[]{:S(2)}) collective-permute-start(bf16[256,1,256]{2,0,1:T(8,128)(2,1)S(1)} %bitcast.924), channel_id=1, source_target_pairs={{0,1},{1,2},{2,3},{3,4},{4,5},{5,6},{6,7},{7,8},{8,9},{9,10},{10,1... | collective-permute-start | bytes 393224 | tf_op jit(solution)/shard_map/ppermute | solution.py:21
  6.1 26.9 %collective-permute-start = (bf16[256,1,256]{2,0,1:T(8,128)(2,1)S(1)}, bf16[256,1,256]{2,0,1:T(8,128)(2,1)S(1)}, u32[]{:S(2)}, u32[]{:S(2)}) collective-permute-start(bf16[256,1,256]{2,0,1:T(8,128)(2,1)S(1)} %bitcast.925), channel_id=1, source_target_pairs={{1,0},{2,1},{3,2},{4,3},{5,4},{6,5},{7,6},{8,7},{9,8},{10,9},{11,1... | collective-permute-start | bytes 393224 | tf_op jit(solution)/shard_map/ppermute | solution.py:23
  9.4 9.2 %collective-permute-start.6 = (bf16[128,1,256]{0,2,1:T(8,128)(2,1)S(1)}, bf16[128,1,256]{0,2,1:T(8,128)(2,1)S(1)}, u32[]{:S(2)}, u32[]{:S(2)}) collective-permute-start(bf16[128,1,256]{0,2,1:T(8,128)(2,1)S(1)} %bitcast.935), channel_id=1, source_target_pairs={{0,1},{1,2},{2,3},{3,4},{4,5},{5,6},{6,7},{7,8},{8,9},{9,10},{10,1... | collective-permute-start | bytes 196616 | tf_op jit(solution)/shard_map/ppermute | solution.py:21
  13.6 15.0 %collective-permute-start.7 = (bf16[128,1,256]{0,2,1:T(8,128)(2,1)S(1)}, bf16[128,1,256]{0,2,1:T(8,128)(2,1)S(1)}, u32[]{:S(2)}, u32[]{:S(2)}) collective-permute-start(bf16[128,1,256]{0,2,1:T(8,128)(2,1)S(1)} %bitcast.936), channel_id=1, source_target_pairs={{1,0},{2,1},{3,2},{4,3},{5,4},{6,5},{7,6},{8,7},{9,8},{10,9},{11,1... | collective-permute-start | bytes 196616 | tf_op jit(solution)/shard_map/ppermute | solution.py:23
  15.3 33.1 %collective-permute-start.5 = (bf16[64,1,1024]{2,1,0:T(2,128)(2,1)S(1)}, bf16[64,1,1024]{2,1,0:T(2,128)(2,1)S(1)}, u32[]{:S(2)}, u32[]{:S(2)}) collective-permute-start(bf16[64,1,1024]{2,1,0:T(2,128)(2,1)S(1)} %get-tuple-element.93), channel_id=1, source_target_pairs={{1,0},{2,1},{3,2},{4,3},{5,4},{6,5},{7,6},{8,7},{9,8},{10,9},{11,1... | collective-permute-start | bytes 393224 | tf_op jit(solution)/shard_map/ppermute | solution.py:23
  18.6 29.7 %collective-permute-start.4 = (bf16[64,1,1024]{2,1,0:T(2,128)(2,1)S(1)}, bf16[64,1,1024]{2,1,0:T(2,128)(2,1)S(1)}, u32[]{:S(2)}, u32[]{:S(2)}) collective-permute-start(bf16[64,1,1024]{2,1,0:T(2,128)(2,1)S(1)} %get-tuple-element.94), channel_id=1, source_target_pairs={{0,1},{1,2},{2,3},{3,4},{4,5},{5,6},{6,7},{7,8},{8,9},{9,10},{10,1... | collective-permute-start | bytes 393224 | tf_op jit(solution)/shard_map/ppermute | solution.py:21
  31.2 1.9 %copy-start.3 = (bf16[27,128,256]{2,1,0:T(8,128)(2,1)S(1)}, bf16[27,128,256]{2,1,0:T(8,128)(2,1)}, u32[]{:S(2)}) copy-start(bf16[27,128,256]{2,1,0:T(8,128)(2,1)} %param.11) | copy-start | bytes 5308420
  41.8 12.8 %copy-start.1 = (bf16[128,2,1024]{0,2,1:T(8,128)(2,1)}, bf16[128,2,1024]{0,2,1:T(8,128)(2,1)S(1)}, u32[]{:S(2)}) copy-start(bf16[128,2,1024]{0,2,1:T(8,128)(2,1)S(1)} %fusion.81) | copy-start | bytes 1572868
  42.8 96.4 %collective-permute-start.3 = (bf16[128,1,1024]{0,2,1:T(8,128)(2,1)}, bf16[128,1,1024]{0,2,1:T(8,128)(2,1)}, u32[]{:S(2)}, u32[]{:S(2)}) collective-permute-start(bf16[128,1,1024]{0,2,1:T(8,128)(2,1)} %get-tuple-element.52), channel_id=1, source_target_pairs={{0,1},{1,2},{2,3},{3,4},{4,5},{5,6},{6,7},{7,8},{8,9},{9,10},{10,1... | collective-permute-start | bytes 786440 | tf_op jit(solution)/shard_map/ppermute | solution.py:21
  46.8 92.4 %collective-permute-start.2 = (bf16[128,1,1024]{0,2,1:T(8,128)(2,1)}, bf16[128,1,1024]{0,2,1:T(8,128)(2,1)}, u32[]{:S(2)}, u32[]{:S(2)}) collective-permute-start(bf16[128,1,1024]{0,2,1:T(8,128)(2,1)} %get-tuple-element.53), channel_id=1, source_target_pairs={{1,0},{2,1},{3,2},{4,3},{5,4},{6,5},{7,6},{8,7},{9,8},{10,9},{11,1... | collective-permute-start | bytes 786440 | tf_op jit(solution)/shard_map/ppermute | solution.py:23
  144.7 3.5 %copy-start.4 = (bf16[27,64,128]{2,1,0:T(8,128)(2,1)S(1)}, bf16[27,64,128]{2,1,0:T(8,128)(2,1)}, u32[]{:S(2)}) copy-start(bf16[27,64,128]{2,1,0:T(8,128)(2,1)} %param.10) | copy-start | bytes 1327108
  150.9 1.2 copy-start.2
